TPU v7x, 32 devices: a whole 2x2x4 slice. The times are simulated.
32 devices in a mesh: query: 4 (over y, x), corpus: 8 (over z, core).
Axes of the slice: x: 2, y: 2, z: 4, core: 2. Of those that a mesh axis runs over, the one named last changes fastest.
Arguments:
- hidden_in: bfloat16 [512, 4096], P('query', 'corpus'), may hold values from -6 to 6
- lengths: int32 [16], P('query'), may hold values from 1 to 32, 320 in all
- gate_weight: bfloat16 [4096, 14336], P('query', 'corpus'), may hold values from -0.09375 to 0.09375
- up_weight: bfloat16 [4096, 14336], P('query', 'corpus'), may hold values from -0.09375 to 0.09375
- down_weight: bfloat16 [14336, 4096], P('corpus', 'query'), may hold values from -0.04175957 to 0.04175957
- code_weight: bfloat16 [4096, 1024], P('corpus'), may hold values from -0.03125 to 0.03125
- corpus_codes: bfloat16 [16384, 1024], P(('query', 'corpus')), may hold values from -1 to 1, as said below
Outputs:
- top_scores: float32 [16, 100], replicated
Inputs may be any that keep to these rules, and one draw needn't show every extreme that they name: `corpus_codes`: every entry is +1 or -1. `lengths`: at least one query has all 32 slots real.
All inputs are finite; a program needn't handle non-finite values. No bound on the sum of `lengths` on one device may be relied on, other than what follows from the above.
Results may differ from a plain program's by a relative error of at most 0.00067.
Values may be sent and summed in bfloat16 or wider, within the bound.
A program may use at most 128 MiB of HBM per device.

v0:
```python
import math

import jax
import jax.numpy as jnp
from jax import lax
from jax.sharding import PartitionSpec as P

D = 4096
SEQ = 32
TOPK = 100


epsilon = 1e-05


def combined_all(value, axis, join):
    pieces = lax.all_gather(value, axis)
    head = pieces[0]
    tail = pieces[1:]
    running, _ = lax.scan(lambda running, section: (join(running, section), None), head, tail)
    return running


def keep_best(first, second):
    return lax.top_k(jnp.concatenate([first, second], axis=1), first.shape[1])[0]


def per_device(hidden_in, lengths, gate_weight, up_weight, down_weight, code_weight, corpus_codes):
    gathered = lax.all_gather(hidden_in, "corpus", axis=1, tiled=True)
    widened = gathered.astype(jnp.float32)
    normed = (
        widened * lax.rsqrt(jnp.mean(widened * widened, axis=1, keepdims=True) + epsilon)
    ).astype(jnp.bfloat16)
    gate_sum = jnp.dot(
        normed,
        lax.all_gather(gate_weight, "query", axis=0, tiled=True),
        preferred_element_type=jnp.float32,
    )
    up_sum = jnp.dot(
        normed,
        lax.all_gather(up_weight, "query", axis=0, tiled=True),
        preferred_element_type=jnp.float32,
    )
    hidden_units = (jax.nn.silu(gate_sum) * up_sum).astype(jnp.bfloat16)
    branch_part = jnp.dot(
        hidden_units,
        lax.all_gather(down_weight, "query", axis=1, tiled=True),
        preferred_element_type=jnp.float32,
    )
    feat_width = hidden_in.shape[1]
    branch_out = lax.psum_scatter(branch_part, "corpus", scatter_dimension=1, tiled=True)
    residual = hidden_in.astype(jnp.float32) + branch_out
    total_sq = lax.psum(jnp.sum(residual * residual, axis=1), "corpus")
    final_rows = residual * lax.rsqrt(total_sq / D + epsilon)[:, None]
    group_count = lengths.shape[0]
    grouped = final_rows.reshape(group_count, SEQ, feat_width)
    valid_mask = (jnp.arange(SEQ, dtype=jnp.int32)[None, :] < lengths[:, None]).astype(jnp.float32)
    pooled = jnp.sum(grouped * valid_mask[:, :, None], axis=1) / lengths[:, None].astype(
        jnp.float32
    )
    pooled = pooled.astype(jnp.bfloat16)
    code_part = jnp.dot(pooled, code_weight, preferred_element_type=jnp.float32)
    group_codes = lax.psum(code_part, "corpus").astype(jnp.bfloat16)
    query_codes = lax.all_gather(group_codes, "query", axis=0, tiled=True)
    scale = 1.0 / math.sqrt(corpus_codes.shape[1])
    scores = (
        lax.dot_general(
            query_codes, corpus_codes, (((1,), (1,)), ((), ())), preferred_element_type=jnp.float32
        )
        * scale
    )
    local_best = lax.top_k(scores, TOPK)[0]
    received = lax.all_to_all(local_best, "query", split_axis=0, concat_axis=1, tiled=True)
    group_best = lax.top_k(received, TOPK)[0]
    group_best = combined_all(group_best, "corpus", keep_best)
    top_scores = lax.all_gather(group_best, "query", axis=0, tiled=True)
    return top_scores


def solution(mesh):
    in_specs = (
        P("query", "corpus"),
        P("query"),
        P("query", "corpus"),
        P("query", "corpus"),
        P("corpus", "query"),
        P("corpus", None),
        P(("query", "corpus"), None),
    )
    out_specs = P()
    return jax.shard_map(
        per_device, mesh=mesh, in_specs=in_specs, out_specs=out_specs, check_vma=False
    )
```

profile of v0, /device:TPU:0, one launch (start us, length us, event | category | flops | bytes accessed | tf_op | source)
XLA Modules:
  0.0 629.5 jit_solution(4346916005370233112)
XLA Ops:
  6.5 0.7 all-gather.9.cloned.1.call-update
  7.3 0.0 all-gather.11.cloned.1.call-start
  7.3 0.7 all-gather.11.cloned.1.call-update
  8.0 0.0 all-gather.13.cloned.1.call-start
  8.1 0.7 all-gather.13.cloned.1.call-update
  8.7 0.0 all-gather.15.cloned.1.call-start
  8.8 0.5 all-gather.15.cloned.1.call-update
  9.3 0.0 reduce-scatter.2.cloned.1.call-start
  9.4 24.6 %all-gather.9.cloned.1.call-done = bf16[128,4096]{1,0:T(8,128)(2,1)} async-done(((bf16[128,512]{1,0:T(8,128)(2,1)}), bf16[128,4096]{1,0:T(8,128)(2,1)}) %all-gather.9.cloned.1.call-update) | async-done | bytes 1048592 | tf_op jit(solution)/shard_map/all_gather | solution.py:29
  33.9 1.6 fusion.1
  35.6 139.7 %all-gather.11.cloned.1.call-done = bf16[4096,1792]{1,0:T(8,128)(2,1)} async-done(((bf16[1024,1792]{1,0:T(8,128)(2,1)}), bf16[4096,1792]{1,0:T(8,128)(2,1)}) %all-gather.11.cloned.1.call-update) | async-done | bytes 14680080 | tf_op jit(solution)/shard_map/all_gather | solution.py:36
  175.2 7.6 %fusion.7 = f32[128,1792]{1,0:T(8,128)S(1)} fusion(bf16[4096,1792]{1,0:T(8,128)(2,1)} %all-gather.11.cloned.1.call-done, bf16[128,4096]{1,0:T(8,128)(2,1)} %all-gather.9.cloned.1.call-done, f32[128]{0:T(128)S(1)} %add_rsqrt_fusion.1), kind=kOutput, calls=%fused_computation.11 | convolution fusion | flops 1880621056 | bytes 16646656 | tf_op jit(solution)/shard_map/dot_general | solution.py:34
  182.9 134.1 %all-gather.13.cloned.1.call-done = bf16[4096,1792]{1,0:T(8,128)(2,1)} async-done(((bf16[1024,1792]{1,0:T(8,128)(2,1)}), bf16[4096,1792]{1,0:T(8,128)(2,1)}) %all-gather.13.cloned.1.call-update) | async-done | bytes 14680080 | tf_op jit(solution)/shard_map/all_gather | solution.py:41
  317.0 141.6 %all-gather.15.cloned.1.call-done = bf16[1792,4096]{1,0:T(8,128)(2,1)} async-done(((bf16[1792,1024]{1,0:T(8,128)(2,1)}), bf16[1792,4096]{1,0:T(8,128)(2,1)}) %all-gather.15.cloned.1.call-update) | async-done | bytes 14680080 | tf_op jit(solution)/shard_map/all_gather | solution.py:47
  458.5 15.1 %fusion.3 = f32[128,4096]{1,0:T(8,128)} fusion(bf16[1792,4096]{1,0:T(8,128)(2,1)} %all-gather.15.cloned.1.call-done, bf16[4096,1792]{1,0:T(8,128)(2,1)} %all-gather.13.cloned.1.call-done, f32[128,1792]{1,0:T(8,128)S(1)} %fusion.7, bf16[128,4096]{1,0:T(8,128)(2,1)S(1)} %copy-done.1, f32[128]{0:T(128)S(1)} %add_rsqrt_fusion.1), kind=kOutput, calls=%fused_computation.9 | convolution fusion | flops 3761045504 | bytes 33423872 | tf_op jit(solution)/shard_map/dot_general | solution.py:45
  473.7 0.0 reduce-scatter.2.cloned.1.call-update
  473.7 0.1 fusion.12
  473.8 36.1 %reduce-scatter.2.cloned.1.call-done = f32[128,512]{1,0:T(8,128)} async-done(((f32[128,4096]{1,0:T(8,128)}), f32[128,512]{1,0:T(8,128)}) %reduce-scatter.2.cloned.1.call-update) | async-done | bytes 262160 | tf_op jit(solution)/shard_map/reduce_scatter | solution.py:51
  509.9 1.1 multiply_reduce_fusion.1
  511.0 14.5 %psum.14 = f32[128]{0:T(128)S(1)} all-reduce(f32[128]{0:T(128)S(1)} %multiply_reduce_fusion.1), channel_id=1, replica_groups=mesh['query'=4,'corpus'=8] {'corpus'}, use_global_device_ids=true, to_apply=%region_3.4 | all-reduce | flops 128 | bytes 1024 | tf_op jit(solution)/shard_map/psum | solution.py:53
  525.6 1.1 multiply_reduce_fusion
  526.6 1.5 fusion.10
  528.1 25.9 %psum.15 = bf16[4,1024]{1,0:T(4,128)(2,1)S(1)} all-reduce(f32[4,1024]{1,0:T(4,128)S(1)} %fusion.10), channel_id=1, replica_groups=mesh['query'=4,'corpus'=8] {'corpus'}, use_global_device_ids=true, to_apply=%region_5.6 | all-reduce | flops 4096 | bytes 24576 | tf_op jit(solution)/shard_map/psum | solution.py:63
  554.1 8.2 %all-gather.1 = bf16[4,4,1024]{2,1,0:T(4,128)(2,1)S(1)} all-gather(bf16[1,4,1024]{2,1,0:T(4,128)(2,1)S(1)} %bitcast.24), channel_id=1, replica_groups=mesh['query'=4,'corpus'=8] {'query'}, dimensions={0}, use_global_device_ids=true | all-gather | bytes 40960 | tf_op jit(solution)/shard_map/all_gather | solution.py:64
  562.2 0.4 convolution_multiply_fusion.1
  562.6 3.8 sort_prefixfusion
  566.4 3.2 all-to-all-start
  569.6 4.7 all-to-all-done
  574.3 0.1 all_to_all.17
  574.4 4.1 top_k.25
  578.5 12.8 %all-gather.2 = f32[8,4,100]{2,1,0:T(4,128)S(1)} all-gather(f32[1,4,100]{2,1,0:T(4,128)S(1)} %slice_bitcast_fusion.1), channel_id=2, replica_groups=mesh['query'=4,'corpus'=8] {'corpus'}, dimensions={0}, use_global_device_ids=true | all-gather | bytes 14400 | tf_op jit(solution)/shard_map/all_gather | solution.py:17
  591.2 24.0 %while.10 = (s32[]{:T(128)}, f32[4,100]{1,0:T(4,128)S(1)}, f32[7,4,100]{2,1,0:T(4,128)S(1)}, s32[]{:T(128)}) while((s32[]{:T(128)}, f32[4,100]{1,0:T(4,128)S(1)}, f32[7,4,100]{2,1,0:T(4,128)S(1)}, s32[]{:T(128)}) %tuple.18), condition=%wide.region_10.11_spmd, body=%wide.region_8.10_spmd.sunk | while | flops 8802 | bytes 28857 | solution.py:20
  591.2 0.1 pad_maximum_fusion.2
  591.3 3.3 top_k.48
  594.6 0.1 pad_maximum_fusion.2
  594.7 3.3 top_k.48
  598.1 0.1 pad_maximum_fusion.2
  598.2 3.3 top_k.48
  601.5 0.1 pad_maximum_fusion.2
  601.6 3.3 top_k.48
  604.9 0.1 pad_maximum_fusion.2
  605.0 3.3 top_k.48
  608.4 0.1 pad_maximum_fusion.2
  608.4 3.3 top_k.48
  611.8 0.1 pad_maximum_fusion.2
  611.9 3.3 top_k.48
  615.2 7.2 %all-gather.3 = f32[4,4,100]{2,1,0:T(4,128)S(1)} all-gather(f32[1,4,100]{2,1,0:T(4,128)S(1)} %bitcast.23), channel_id=1, replica_groups=mesh['query'=4,'corpus'=8] {'query'}, dimensions={0}, use_global_device_ids=true | all-gather | bytes 8000 | tf_op jit(solution)/shard_map/all_gather | solution.py:76
  622.4 0.6 copy.19
  (39 shorter events, 0.1 us)
Async XLA Ops:
  6.5 555.7 %copy-start = (bf16[512,1024]{1,0:T(8,128)(2,1)S(1)}, bf16[512,1024]{1,0:T(8,128)(2,1)}, u32[]{:S(2)}) copy-start(bf16[512,1024]{1,0:T(8,128)(2,1)} %param.15) | copy-start | bytes 3145732
  6.5 27.4 %all-gather.9.cloned.1.call-start = ((), (), s32[]{:S(2)}) async-start(), calls=%async_computation.2 | async-start | bytes 1179648 | tf_op jit(solution)/shard_map/all_gather | solution.py:29
  7.3 168.0 %all-gather.11.cloned.1.call-start = ((), (), s32[]{:S(2)}) async-start(), calls=%async_computation.3 | async-start | bytes 18350080 | tf_op jit(solution)/shard_map/all_gather | solution.py:36
  8.0 309.0 %all-gather.13.cloned.1.call-start = ((), (), s32[]{:S(2)}) async-start(), calls=%async_computation.4 | async-start | bytes 18350080 | tf_op jit(solution)/shard_map/all_gather | solution.py:41
  8.7 449.8 %all-gather.15.cloned.1.call-start = ((), (), s32[]{:S(2)}) async-start(), calls=%async_computation.5 | async-start | bytes 18350080 | tf_op jit(solution)/shard_map/all_gather | solution.py:47
  9.3 500.6 %reduce-scatter.2.cloned.1.call-start = ((), (), s32[]{:S(2)}) async-start(), calls=%async_computation.6 | async-start | bytes 2359296 | tf_op jit(solution)/shard_map/reduce_scatter | solution.py:51
  33.9 424.6 %copy-start.1 = (bf16[128,4096]{1,0:T(8,128)(2,1)S(1)}, bf16[128,4096]{1,0:T(8,128)(2,1)}, u32[]{:S(2)}) copy-start(bf16[128,4096]{1,0:T(8,128)(2,1)} %all-gather.9.cloned.1.call-done) | copy-start | bytes 3145732
  182.9 290.8 %copy-start.3 = (s32[4]{0:T(128)S(1)}, s32[4]{0:T(128)}, u32[]{:S(2)}) copy-start(s32[4]{0:T(128)} %param.10) | copy-start | bytes 52
  182.9 327.1 %copy-start.2 = (bf16[128,512]{1,0:T(8,128)(2,1)S(1)}, bf16[128,512]{1,0:T(8,128)(2,1)}, u32[]{:S(2)}) copy-start(bf16[128,512]{1,0:T(8,128)(2,1)} %param.9) | copy-start | bytes 393220
  566.4 7.9 %all-to-all-start = ((f32[4,4,100]{2,1,0:T(4,128)}), f32[4,4,100]{2,1,0:T(4,128)S(1)}, u32[]{:S(2)}, u32[]{:S(2)}) async-start(f32[4,4,100]{2,1,0:T(4,128)} %bitcast.3), calls=%async_computation.1 | async-start | bytes 16384 | tf_op jit(solution)/shard_map/all_to_all | solution.py:73
Sparse Core Ops, SparseCore 0:
  8.9 24.9 all-gather.8
  35.8 139.4 all-gather.10
  177.1 139.8 all-gather.12
  318.7 139.8 all-gather.14
  473.8 36.0 reduce-scatter.1
where the time goes:
time: 630 us; the launch traced here: 629 us
  waiting for transfers between devices  483 us (77%)
  blocking collectives  68.5 us (11%)
  other arithmetic  35.6 us (6%)
  matrix products  24.6 us (4%)
  between operations  13.2 us (2%)
    all_gather x1, waiting for transfers between devices, per_device(): lax.all_gather(down_weight, 'query', axis=1, tiled=True)  142 us
    all_gather x1, waiting for transfers between devices, per_device(): lax.all_gather(gate_weight, 'query', axis=0, tiled=True)  140 us
    all_gather x1, waiting for transfers between devices, per_device(): lax.all_gather(up_weight, 'query', axis=0, tiled=True)  134 us
    reduce_scatter x1, waiting for transfers between devices, per_device(): lax.psum_scatter(branch_part, 'corpus', scatter_dimension=1, tiled=True)  36.1 us
    psum x1, blocking collectives, per_device(): group_codes = lax.psum(code_part, 'corpus').astype(jnp.bfloat16)  25.9 us
    all_gather x1, waiting for transfers between devices, per_device(): gathered = lax.all_gather(hidden_in, 'corpus', axis=1, tiled=True)  24.6 us
    top_k x7, other arithmetic, keep_best(): lax.top_k(jnp.concatenate([first, second], axis=1), first.shape[1])[0]  23.4 us
    dot_general x1, matrix products, per_device(): jnp.dot(hidden_units, lax.all_gather(down_weight, 'query', axis=1, tiled=...  15.1 us
  transfers between devices with their start and end apart: 6, of which 6 were waited for; matrix products, arithmetic and copies ran while one was open for 1% of the time, Pallas kernels for 0%

commit v1 on v0

v1 whole, which is shorter than its diff:
```python
import functools
import math

import jax
import jax.numpy as jnp
from jax import lax
from jax.experimental import pallas as pl
from jax.experimental.pallas import tpu as pltpu
from jax.sharding import PartitionSpec as P

SEQ = 32
TOPK = 100
REAL_NUM, REAL_DEN = 5, 8
CHUNK = 256

epsilon = 1e-05
F32, BF16 = jnp.float32, jnp.bfloat16


def mm(a, b, precision=None):
    return lax.dot_general(a, b, (((1,), (0,)), ((), ())), precision=precision, preferred_element_type=F32)


def rcopy(src, dst, send, recv, dev):
    return pltpu.make_async_remote_copy(
        src_ref=src, dst_ref=dst, send_sem=send, recv_sem=recv,
        device_id=dev, device_id_type=pl.DeviceIdType.MESH)


def block_kernel(dims, hid, lens, gate_h, up_h, down_h, code_h, corp_h, out,
                 gate, up, down, code, corp, colbuf, lens_all, xall, psend, precv,
                 ss_send, ss_recv, hall, acc, lsend, lrecv, gsend, grecv, t_send, t_recv,
                 pp, prc, pblk, cpart, crecv, codes,
                 w_s, a_s, a_r, l_s, l_r, ch_s, ch_r, la_s, la_r, p_s, p_r, ss_s, ss_r, h_s, h_r,
                 lr_s, lr_r, g_s, g_r, t_s, t_r, pp_s, pp_r, pb_s, pb_r, c_s, c_r, o_s, o_r):
    nq, nc, r, nreal, tq, tb, nch, cw, d_all = dims
    q = lax.axis_index("query")
    c = lax.axis_index("corpus")
    g = c // r
    j = lax.rem(c, r)
    slots, w = hid.shape[0], hid.shape[1]
    total = nq * slots
    nqueries = total // SEQ
    bw = code.shape[1] // nq

    loads = []
    for i, (s, d) in enumerate(((gate_h, gate), (up_h, up), (down_h, down), (code_h, code), (corp_h, corp))):
        cp = pltpu.make_async_copy(s, d, w_s.at[i])
        cp.start()
        loads.append(cp)

    def rq(k):
        return lax.rem(q + k, nq)

    def rc(k):
        return lax.rem(c + k, nc)

    def lane(k):
        return lax.rem(j + k, r)

    barrier = pltpu.get_barrier_semaphore()
    for k in range(1, nq):
        pl.semaphore_signal(barrier, inc=1, device_id=(rq(k), c), device_id_type=pl.DeviceIdType.MESH)
    for k in range(1, nc):
        pl.semaphore_signal(barrier, inc=1, device_id=(q, rc(k)), device_id_type=pl.DeviceIdType.MESH)
    pl.semaphore_wait(barrier, nq - 1 + nc - 1)

    for k in range(1, nq):
        rcopy(lens, lens_all.at[q], l_s.at[k], l_r.at[q], (rq(k), c)).start()

    @pl.when(q != g)
    def _():
        rcopy(hid, colbuf.at[q], a_s, a_r.at[q], (g, c)).start()

    lens_all[q] = lens[...]
    for k in range(1, nq):
        s = rq(k)
        rcopy(lens, lens_all.at[s], l_s.at[k], l_r.at[s], (s, c)).wait_recv()
    lens_row = jnp.concatenate([lens_all[i] for i in range(nq)], axis=1)
    slot = lax.broadcasted_iota(jnp.int32, (8, total), 1)
    valid = lax.rem(slot, SEQ) < lens_row
    before = lax.broadcasted_iota(jnp.int32, (total, total), 0) < lax.broadcasted_iota(jnp.int32, (total, total), 1)
    pos = mm(valid.astype(F32).astype(BF16), before.astype(F32).astype(BF16)).astype(jnp.int32)
    pos = jnp.where(valid, pos, -1)[:1]

    def chunk(i, slot_j):
        return xall.at[slot_j, pl.ds(i * tq, tq)]

    def down_chain(i):
        return rcopy(chunk(i, j), chunk(i, j), ch_s.at[0, i], ch_r.at[i], (q, jnp.maximum(c - r, 0)))

    def up_chain(i):
        return rcopy(chunk(i, j), chunk(i, j), ch_s.at[1, i], ch_r.at[i], (q, jnp.minimum(c + r, nc - 1)))

    sends_up = jnp.logical_and(g >= q, g < nc // r - 1)
    sends_down = jnp.logical_and(g <= q, g > 0)

    @pl.when(q == g)
    def _():
        colbuf[q] = hid[...]
        for k in range(1, nq):
            s = rq(k)
            rcopy(hid, colbuf.at[s], a_s, a_r.at[s], (s, c)).wait_recv()
        stacked = colbuf[...].reshape(total, w)
        for i in range(nq):
            row = lax.broadcasted_iota(jnp.int32, (tq, total), 0) + i * tq
            pick = (pos == row).astype(F32).astype(BF16)
            xall[j, i * tq:(i + 1) * tq, :] = mm(pick, stacked).astype(BF16)

    for i in range(nq):
        @pl.when(q != g)
        def _(i=i):
            up_chain(i).wait_recv()

        @pl.when(sends_up)
        def _(i=i):
            up_chain(i).start()

        @pl.when(sends_down)
        def _(i=i):
            down_chain(i).start()

        for k in range(1, r):
            rcopy(chunk(i, j), chunk(i, j), la_s.at[k, i], la_r.at[j, i], (q, g * r + lane(k))).start()
    for i in range(nq):
        for k in range(1, r):
            s = lane(k)
            rcopy(chunk(i, s), chunk(i, s), la_s.at[k, i], la_r.at[s, i], (q, g * r + s)).wait_recv()

    loads[0].wait()
    loads[1].wait()

    sq = sum(jnp.sum(jnp.square(xall[i].astype(F32)), axis=1, keepdims=True) for i in range(r))
    for i in range(nq):
        ss_send[i] = jnp.broadcast_to(sq[i * tq:(i + 1) * tq], (tq, 128))
    for k in range(1, nq):
        d = rq(k)
        rcopy(ss_send.at[d], ss_recv.at[q], ss_s.at[k], ss_r.at[q], (d, c)).start()

    def part_send(n, k):
        d = rq(k)
        return rcopy(psend.at[n, d], precv.at[n, q], p_s.at[n, k], p_r.at[n, q], (d, c))

    def part_recv(n, k):
        s = rq(k)
        return rcopy(psend.at[n, s], precv.at[n, s], p_s.at[n, k], p_r.at[n, s], (s, c))

    def h_send(n, k):
        return rcopy(hall.at[n, q], hall.at[n, q], h_s.at[n, k], h_r.at[n, q], (rq(k), c))

    def h_recv(n, k):
        s = rq(k)
        return rcopy(hall.at[n, s], hall.at[n, s], h_s.at[n, k], h_r.at[n, s], (s, c))

    def matmuls(n, carry):
        cols = pl.ds(pl.multiple_of(n * cw, cw), cw)
        for e, wref in enumerate((gate, up)):
            full = sum(mm(xall[i], wref[i * w:(i + 1) * w, cols]) for i in range(r)).astype(BF16)
            for i in range(nq):
                psend[n, i, e] = full[i * tq:(i + 1) * tq]
        for k in range(1, nq):
            part_send(n, k).start()
        return carry

    lax.fori_loop(0, nch, matmuls, 0)

    ssum = ss_send[q]
    for k in range(1, nq):
        s = rq(k)
        rcopy(ss_send.at[s], ss_recv.at[s], ss_s.at[k], ss_r.at[s], (s, c)).wait_recv()
        ssum = ssum + ss_recv[s]
    inv = lax.rsqrt(ssum[:, :1] / d_all + epsilon)
    loads[2].wait()
    acc[...] = jnp.zeros_like(acc)

    def reduce_chunk(n):
        gsum = psend[n, q, 0].astype(F32)
        usum = psend[n, q, 1].astype(F32)
        for k in range(1, nq):
            part_recv(n, k).wait_recv()
            s = rq(k)
            gsum = gsum + precv[n, s, 0].astype(F32)
            usum = usum + precv[n, s, 1].astype(F32)
        gsum = gsum * inv
        usum = usum * inv
        hall[n, q] = (gsum / (1.0 + jnp.exp(-gsum)) * usum).astype(BF16)
        for k in range(1, nq):
            h_send(n, k).start()

    def down_chunk(n):
        for k in range(1, nq):
            h_recv(n, k).wait_recv()
        acc[...] += mm(hall[n].reshape(nreal, cw), down[pl.ds(pl.multiple_of(n * cw, cw), cw), :])

    reduce_chunk(0)

    def both(n, carry):
        reduce_chunk(n)
        down_chunk(n - 1)
        return carry

    lax.fori_loop(1, nch, both, 0)
    down_chunk(nch - 1)

    ng = nc // r
    for gg in range(ng):
        for jj in range(r):
            b = gg * r + jj
            lsend[jj, gg] = acc[b * tb:(b + 1) * tb].astype(BF16)
    for k in range(1, r):
        t = lane(k)
        rcopy(lsend.at[t], lrecv.at[j], lr_s.at[k], lr_r.at[j], (q, g * r + t)).start()
    mine = lsend[j].astype(F32)
    for k in range(1, r):
        s = lane(k)
        rcopy(lsend.at[s], lrecv.at[s], lr_s.at[k], lr_r.at[s], (q, g * r + s)).wait_recv()
        mine = mine + lrecv[s].astype(F32)
    gsend[...] = mine.astype(BF16)
    for k in range(1, ng):
        t = lax.rem(g + k, ng)
        rcopy(gsend.at[t], grecv.at[g], g_s.at[k], g_r.at[g], (q, t * r + j)).start()
    row = lax.broadcasted_iota(jnp.int32, (tb, nreal), 0) + c * tb
    own_rows = (lax.broadcasted_iota(jnp.int32, (tb, nreal), 1) == row).astype(F32).astype(BF16)
    residual = jnp.concatenate([mm(own_rows, xall[i]) for i in range(r)], axis=1)
    residual = residual + gsend[g].astype(F32)
    for k in range(1, ng):
        s = lax.rem(g + k, ng)
        rcopy(gsend.at[s], grecv.at[s], g_s.at[k], g_r.at[s], (q, s * r + j)).wait_recv()
        residual = residual + grecv[s].astype(F32)

    t_send[...] = jnp.broadcast_to(jnp.sum(residual * residual, axis=1, keepdims=True), (tb, 128))
    for k in range(1, nq):
        rcopy(t_send, t_recv.at[q], t_s.at[k], t_r.at[q], (rq(k), c)).start()
    qrow = lax.broadcasted_iota(jnp.int32, (nqueries, total), 0)
    qslot = lax.broadcasted_iota(jnp.int32, (nqueries, total), 1)
    lens_b = jnp.broadcast_to(lens_row[:1], (nqueries, total)).astype(F32)
    vals_b = jnp.broadcast_to(valid.astype(F32)[:1], (nqueries, total))
    len_col = jnp.sum(jnp.where(qslot == qrow * SEQ, lens_b, 0.0), axis=1, keepdims=True)
    off_col = jnp.sum(jnp.where(qslot < qrow * SEQ, vals_b, 0.0), axis=1, keepdims=True)
    prow = (lax.broadcasted_iota(jnp.int32, (nqueries, tb), 1) + c * tb).astype(F32)
    member = jnp.where(jnp.logical_and(prow >= off_col, prow < off_col + len_col), 1.0, 0.0)
    tsum = t_send[...]
    for k in range(1, nq):
        s = rq(k)
        rcopy(t_send, t_recv.at[s], t_s.at[k], t_r.at[s], (s, c)).wait_recv()
        tsum = tsum + t_recv[s]
    final = residual * lax.rsqrt(tsum[:, :1] / d_all + epsilon)
    pooled_part = mm(member, final, lax.Precision.HIGHEST)
    for i in range(r):
        pp[i] = pooled_part[:, i * w:(i + 1) * w]
    for i in range(r):
        @pl.when(c != q * r + i)
        def _(i=i):
            rcopy(pp.at[i], prc.at[c], pp_s.at[i], pp_r.at[c], (q, q * r + i)).start()

    @pl.when(g == q)
    def _():
        pooled = pp[j]
        for k in range(1, nc):
            s = rc(k)
            rcopy(pp.at[j], prc.at[s], pp_s.at[0], pp_r.at[s], (q, s)).wait_recv()
            pooled = pooled + prc[s]
        pblk[...] = (pooled / len_col).astype(BF16)
        for k in range(1, nq):
            rcopy(pblk, pblk, pb_s.at[k], pb_r, (rq(k), c)).start()

    loads[3].wait()
    loads[4].wait()

    @pl.when(g != q)
    def _():
        rcopy(pblk, pblk, pb_s.at[0], pb_r, (g, c)).wait_recv()

    cpart[...] = mm(pblk[...], code[:, pl.ds(pl.multiple_of(q * bw, bw), bw)])
    for k in range(1, nc):
        rcopy(cpart, crecv.at[c], c_s.at[k], c_r.at[c], (q, rc(k))).start()
    crecv[c] = cpart[...]
    for k in range(1, nc):
        s = rc(k)
        rcopy(cpart, crecv.at[s], c_s.at[k], c_r.at[s], (q, s)).wait_recv()
    csum = crecv[0]
    for i in range(1, nc):
        csum = csum + crecv[i]
    codes[q] = csum.astype(BF16)
    for k in range(1, nq):
        rcopy(codes.at[q], codes.at[q], o_s.at[k], o_r.at[q], (rq(k), c)).start()
    for k in range(1, nq):
        s = rq(k)
        rcopy(codes.at[s], codes.at[s], o_s.at[k], o_r.at[s], (s, c)).wait_recv()
    qcodes = jnp.concatenate([codes[i] for i in range(nq)], axis=1)
    scale = 1.0 / math.sqrt(corp.shape[1])
    out[...] = lax.dot_general(qcodes, corp[...], (((1,), (1,)), ((), ())), preferred_element_type=F32) * scale

    for k in range(1, nq):
        rcopy(lens, lens_all.at[q], l_s.at[k], l_r.at[q], (rq(k), c)).wait_send()
        rcopy(ss_send.at[q], ss_recv.at[q], ss_s.at[k], ss_r.at[q], (rq(k), c)).wait_send()
        rcopy(t_send, t_recv.at[q], t_s.at[k], t_r.at[q], (rq(k), c)).wait_send()
        rcopy(codes.at[q], codes.at[q], o_s.at[k], o_r.at[q], (rq(k), c)).wait_send()

    @pl.when(q != g)
    def _():
        rcopy(hid, colbuf.at[q], a_s, a_r.at[q], (g, c)).wait_send()

    for i in range(nq):
        @pl.when(sends_up)
        def _(i=i):
            up_chain(i).wait_send()

        @pl.when(sends_down)
        def _(i=i):
            down_chain(i).wait_send()

        for k in range(1, r):
            rcopy(chunk(i, j), chunk(i, j), la_s.at[k, i], la_r.at[j, i], (q, g * r + lane(k))).wait_send()

    def drain(n, carry):
        for k in range(1, nq):
            part_send(n, k).wait_send()
            h_send(n, k).wait_send()
        return carry

    lax.fori_loop(0, nch, drain, 0)
    for k in range(1, r):
        rcopy(lsend.at[lane(k)], lrecv.at[j], lr_s.at[k], lr_r.at[j], (q, g * r + lane(k))).wait_send()
    for k in range(1, ng):
        t = lax.rem(g + k, ng)
        rcopy(gsend.at[t], grecv.at[g], g_s.at[k], g_r.at[g], (q, t * r + j)).wait_send()
    for i in range(r):
        @pl.when(c != q * r + i)
        def _(i=i):
            rcopy(pp.at[i], prc.at[c], pp_s.at[i], pp_r.at[c], (q, q * r + i)).wait_send()

    @pl.when(g == q)
    def _():
        for k in range(1, nq):
            rcopy(pblk, pblk, pb_s.at[k], pb_r, (rq(k), c)).wait_send()
    for k in range(1, nc):
        rcopy(cpart, crecv.at[c], c_s.at[k], c_r.at[c], (q, rc(k))).wait_send()


def device_scores(nq, nc, hidden_in, lengths, gate_weight, up_weight, down_weight, code_weight, corpus_codes):
    slots, w = hidden_in.shape
    r = nc // nq
    nreal = nq * slots * REAL_NUM // REAL_DEN
    tq, tb = nreal // nq, nreal // nc
    dq, ffc = gate_weight.shape
    cw = CHUNK if ffc % CHUNK == 0 else ffc
    nch = ffc // cw
    nqueries = nq * lengths.shape[0]
    bits = code_weight.shape[1]
    bw = bits // nq
    ng = nc // r
    lens = jnp.broadcast_to(jnp.repeat(lengths, SEQ)[None, :], (8, slots))
    vm, dma = pltpu.VMEM, pltpu.SemaphoreType.DMA
    scratch = [
        vm(gate_weight.shape, BF16), vm(up_weight.shape, BF16), vm(down_weight.shape, BF16),
        vm(code_weight.shape, BF16), vm(corpus_codes.shape, BF16),
        vm((nq, slots, w), BF16), vm((nq, 8, slots), jnp.int32), vm((r, nreal, w), BF16),
        vm((nch, nq, 2, tq, cw), BF16), vm((nch, nq, 2, tq, cw), BF16),
        vm((nq, tq, 128), F32), vm((nq, tq, 128), F32), vm((nch, nq, tq, cw), BF16), vm((nreal, dq), F32),
        vm((r, ng, tb, dq), BF16), vm((r, ng, tb, dq), BF16), vm((ng, tb, dq), BF16), vm((ng, tb, dq), BF16),
        vm((tb, 128), F32), vm((nq, tb, 128), F32),
        vm((r, nqueries, w), F32), vm((nc, nqueries, w), F32), vm((nqueries, w), BF16),
        vm((nqueries, bw), F32), vm((nc, nqueries, bw), F32), vm((nq, nqueries, bw), BF16),
        dma((5,)), dma, dma((nq,)), dma((nq,)), dma((nq,)), dma((2, nq)), dma((nq,)), dma((r, nq)), dma((r, nq)),
        dma((nch, nq)), dma((nch, nq)), dma((nq,)), dma((nq,)), dma((nch, nq)), dma((nch, nq)),
        dma((r,)), dma((r,)), dma((ng,)), dma((ng,)), dma((nq,)), dma((nq,)),
        dma((r,)), dma((nc,)), dma((nq,)), dma, dma((nc,)), dma((nc,)), dma((nq,)), dma((nq,)),
    ]
    dims = (nq, nc, r, nreal, tq, tb, nch, cw, w * nc)
    vspec, aspec = pl.BlockSpec(memory_space=pltpu.VMEM), pl.BlockSpec(memory_space=pl.ANY)
    return pl.pallas_call(
        functools.partial(block_kernel, dims),
        out_shape=jax.ShapeDtypeStruct((nqueries, corpus_codes.shape[0]), F32),
        in_specs=[vspec, vspec] + [aspec] * 5,
        out_specs=vspec,
        scratch_shapes=scratch,
        compiler_params=pltpu.CompilerParams(
            collective_id=0, has_side_effects=True, vmem_limit_bytes=48 * 1024 * 1024),
    )(hidden_in, lens, gate_weight, up_weight, down_weight, code_weight, corpus_codes)


def per_device(nq, nc, *args):
    scores = device_scores(nq, nc, *args)
    local_best = lax.top_k(scores, min(TOPK, scores.shape[1]))[0]
    if nq * nc * local_best.shape[1] > 4096:
        local_best = lax.all_gather(local_best, "query", axis=1, tiled=True)
        local_best = lax.top_k(local_best, TOPK)[0]
        everyone = lax.all_gather(local_best, "corpus", axis=1, tiled=True)
    else:
        everyone = lax.all_gather(local_best, ("query", "corpus"), axis=1, tiled=True)
    return lax.top_k(everyone, TOPK)[0]


def solution(mesh):
    in_specs = (
        P("query", "corpus"),
        P("query"),
        P("query", "corpus"),
        P("query", "corpus"),
        P("corpus", "query"),
        P("corpus", None),
        P(("query", "corpus"), None),
    )
    body = functools.partial(per_device, mesh.shape["query"], mesh.shape["corpus"])
    return jax.shard_map(body, mesh=mesh, in_specs=in_specs, out_specs=P(), check_vma=False)
```

time: 630 us -> 183 us (0.29)
  waiting for transfers between devices: 483 us -> 0 us
  Pallas kernels: 0 us -> 102 us
  blocking collectives: 68.5 us -> 41.7 us
  matrix products: 24.6 us -> 0 us
  between operations: 13.2 us -> 0.03 us
  local copies, waits for them, and re-layouts: 0.79 us -> 7.1 us
    all_gather x4 -> x0, waiting for transfers between devices: 440 us -> none  [the longest x1 142 us: per_device(): lax.all_gather(down_weight, 'query', axis=1, tiled=True)]
    pallas_call x0 -> x1, Pallas kernels: none -> 102 us  [device_scores(): pl.pallas_call(functools.partial(block_kernel, dims), out_shape=jax.Shape...]
    psum x2 -> x0, blocking collectives: 40.4 us -> none  [the longest x1 25.9 us: per_device(): group_codes = lax.psum(code_part, 'corpus').astype(jnp.bfloat16)]
    reduce_scatter x1 -> x0, waiting for transfers between devices: 36.1 us -> none  [per_device(): lax.psum_scatter(branch_part, 'corpus', scatter_dimension=1, tiled=True)]
    dot_general x4 -> x0, matrix products: 24.6 us -> none  [the longest x1 15.1 us: per_device(): jnp.dot(hidden_units, lax.all_gather(down_weight, 'query', axis=1, tiled=...]
    all_gather x3 -> x1, blocking collectives: 28.1 us -> 41.7 us  [per_device(): lax.all_gather(local_best, ('query', 'corpus'), axis=1, tiled=True)]
    top_k x9 -> x2, other arithmetic: 31.2 us -> 31.9 us  [the longest x1 28.8 us: per_device(): return lax.top_k(everyone, TOPK)[0]]
  transfers between devices with their start and end apart: 6 -> 0, of which waited for: 6 -> 0; matrix products, arithmetic and copies ran while one was open for 1% -> 0% of each run, Pallas kernels for 0% -> 0%
where the time goes in v1:
time: 183 us
  Pallas kernels  102 us (56%)
  blocking collectives  41.7 us (23%)
  other arithmetic  31.9 us (17%)
  local copies, waits for them, and re-layouts  7.1 us (4%)
    pallas_call x1, Pallas kernels, device_scores(): pl.pallas_call(functools.partial(block_kernel, dims), out_shape=jax.Shape...  102 us
    all_gather x1, blocking collectives, per_device(): lax.all_gather(local_best, ('query', 'corpus'), axis=1, tiled=True)  41.7 us
    top_k x1, other arithmetic, per_device(): return lax.top_k(everyone, TOPK)[0]  28.8 us
    unnamed x9, local copies, waits for them, and re-layouts  5.58 us

profile of v1, /device:TPU:0, one launch (start us, length us, event | category | flops | bytes accessed | tf_op | source)
XLA Modules:
  0.0 182.5 jit_solution(8173503273758178486)
XLA Ops:
  0.0 0.7 broadcast_in_dim.10
  0.7 0.1 broadcast_in_dim.11
  0.8 0.0 copy-start
  0.8 2.0 %copy-done = bf16[1024,1792]{1,0:T(8,128)(2,1)S(1)} copy-done((bf16[1024,1792]{1,0:T(8,128)(2,1)S(1)}, bf16[1024,1792]{1,0:T(8,128)(2,1)}, u32[]{:S(2)}) %copy-start) | copy-done | bytes 3670040
  2.9 0.0 copy-start.1
  2.9 1.2 copy-done.1
  4.1 0.0 copy-start.2
  4.1 1.2 copy-done.2
  5.3 0.0 copy-start.3
  5.3 0.9 copy-done.3
  6.2 101.8 %shard_map.73 = f32[16,512]{1,0:T(8,128)S(1)} custom-call(bf16[128,512]{1,0:T(8,128)(2,1)S(1)} %copy-done.3, s32[8,128]{1,0:T(8,128)S(1)} %broadcast_in_dim.12.lens, bf16[1024,1792]{1,0:T(8,128)(2,1)S(1)} %copy-done, bf16[1024,1792]{1,0:T(8,128)(2,1)} %up_h.1, bf16[1792,1024]{1,0:T(8,128)(2,1)} %down_h.1, bf16[512,1024]{1,0:T(8,128)(2,1)S(1)} %copy-done.1, ...), custom_call_target="tpu_custom_call" | custom-call | tf_op jit(solution)/shard_map/pallas_call | solution.py:372
  108.0 3.1 %sort_prefixfusion = f32[16,100]{1,0:T(8,128)S(1)} fusion(f32[16,512]{1,0:T(8,128)S(1)} %shard_map.73), kind=kCustom, calls=%top_k.14.sort_prefix | custom fusion | flops 106496 | bytes 39168 | tf_op jit(solution)/shard_map/top_k | solution.py:385
  111.1 41.7 %all-gather = f32[32,100,16]{1,2,0:T(8,128)S(1)} all-gather(f32[1,100,16]{1,2,0:T(8,128)S(1)} %bitcast.7), channel_id=1, replica_groups=mesh['query'=4,'corpus'=8] {'query','corpus'}, dimensions={0}, use_global_device_ids=true | all-gather | bytes 211200 | tf_op jit(solution)/shard_map/all_gather | solution.py:391
  152.8 0.1 copy.8
  152.9 0.2 reshape.2
  153.1 28.8 %top_k.20 = (f32[16,3200]{1,0:T(8,128)S(1)}, s32[16,3200]{1,0:T(8,128)}) sort(f32[16,3200]{1,0:T(8,128)S(1)} %bitcast.6, s32[16,3200]{1,0:T(8,128)S(1)} %iota.7), dimensions={1}, to_apply=%region_1.2 | sort | flops 819200 | bytes 819200 | tf_op jit(solution)/shard_map/top_k | solution.py:392
  181.9 0.6 top_k.21
  (2 shorter events, 0.0 us)
Async XLA Ops:
  0.8 2.0 %copy-start = (bf16[1024,1792]{1,0:T(8,128)(2,1)S(1)}, bf16[1024,1792]{1,0:T(8,128)(2,1)}, u32[]{:S(2)}) copy-start(bf16[1024,1792]{1,0:T(8,128)(2,1)} %gate_h.1) | copy-start | bytes 11010052
  2.9 1.2 copy-start.1
  4.1 1.2 copy-start.2
  5.3 0.9 copy-start.3

commit v2 on v1

--- a/solution.py
+++ b/solution.py
@@ -9,6 +9,7 @@
 from jax.sharding import PartitionSpec as P
 
 SEQ = 32
+LANES = 128
 TOPK = 100
 REAL_NUM, REAL_DEN = 5, 8
 CHUNK = 256
@@ -27,11 +28,49 @@
         device_id=dev, device_id_type=pl.DeviceIdType.MESH)
 
 
+def exchange(x, s, keep_max):
+    bit = (lax.broadcasted_iota(jnp.int32, x.shape, 1) & s) != 0
+    other = jnp.where(bit, pltpu.roll(x, s, 1), pltpu.roll(x, LANES - s, 1))
+    return jnp.where(keep_max, jnp.maximum(x, other), jnp.minimum(x, other))
+
+
+def sort_lanes(x):
+    lane = lax.broadcasted_iota(jnp.int32, x.shape, 1)
+    flip = (lax.broadcasted_iota(jnp.int32, x.shape, 0) >= x.shape[0] // 2).astype(jnp.int32)
+    size = 2
+    while size <= LANES:
+        up = ((lane & size) != 0).astype(jnp.int32) if size < LANES else jnp.zeros_like(lane)
+        s = size // 2
+        while s:
+            low = ((lane & s) != 0).astype(jnp.int32)
+            x = exchange(x, s, (low ^ up ^ flip) == 0)
+            s //= 2
+        size *= 2
+    return x
+
+
+def merge_all(x, rows, lone):
+    while x.shape[0] > rows:
+        half = x.shape[0] // 2
+        x = jnp.maximum(x[:half], x[half:])
+        lane = lax.broadcasted_iota(jnp.int32, x.shape, 1)
+        if half > rows:
+            flip = (lax.broadcasted_iota(jnp.int32, x.shape, 0) >= half // 2).astype(jnp.int32)
+        else:
+            flip = jnp.zeros_like(lane) + jnp.asarray(lone, jnp.int32)
+        s = LANES // 2
+        while s:
+            low = ((lane & s) != 0).astype(jnp.int32)
+            x = exchange(x, s, (low ^ flip) == 0)
+            s //= 2
+    return x
+
+
 def block_kernel(dims, hid, lens, gate_h, up_h, down_h, code_h, corp_h, out,
                  gate, up, down, code, corp, colbuf, lens_all, xall, psend, precv,
-                 ss_send, ss_recv, hall, acc, lsend, lrecv, gsend, grecv, t_send, t_recv,
+                 st_send, st_recv, inv_all, xn, pown, top_q, top_c, hall, acc, lsend, lrecv, gsend, grecv, t_send, t_recv,
                  pp, prc, pblk, cpart, crecv, codes,
-                 w_s, a_s, a_r, l_s, l_r, ch_s, ch_r, la_s, la_r, p_s, p_r, ss_s, ss_r, h_s, h_r,
+                 w_s, a_s, a_r, l_s, l_r, ch_s, ch_r, la_s, la_r, p_s, p_r, st_s, st_r, iv_s, iv_r, tq_s, tq_r, tc_s, tc_r, h_s, h_r,
                  lr_s, lr_r, g_s, g_r, t_s, t_r, pp_s, pp_r, pb_s, pb_r, c_s, c_r, o_s, o_r):
     nq, nc, r, nreal, tq, tb, nch, cw, d_all = dims
     q = lax.axis_index("query")
@@ -72,6 +111,12 @@
     def _():
         rcopy(hid, colbuf.at[q], a_s, a_r.at[q], (g, c)).start()
 
+    squares = jnp.square(hid[...].astype(F32))
+    st_send[...] = lax.dot_general(jnp.ones((8, w), F32), squares, (((1,), (1,)), ((), ())),
+                                   precision=lax.Precision.HIGHEST, preferred_element_type=F32)
+    for k in range(1, nc):
+        rcopy(st_send, st_recv.at[c], st_s.at[k], st_r.at[c], (q, rc(k))).start()
+    st_recv[c] = st_send[...]
     lens_all[q] = lens[...]
     for k in range(1, nq):
         s = rq(k)
@@ -83,6 +128,16 @@
     pos = mm(valid.astype(F32).astype(BF16), before.astype(F32).astype(BF16)).astype(jnp.int32)
     pos = jnp.where(valid, pos, -1)[:1]
 
+    for k in range(1, nc):
+        s = rc(k)
+        rcopy(st_send, st_recv.at[s], st_s.at[k], st_r.at[s], (q, s)).wait_recv()
+    stat = st_recv[0]
+    for i in range(1, nc):
+        stat = stat + st_recv[i]
+    inv_all[q] = lax.rsqrt(stat / d_all + epsilon)
+    for k in range(1, nq):
+        rcopy(inv_all.at[q], inv_all.at[q], iv_s.at[k], iv_r.at[q], (rq(k), c)).start()
+
     def chunk(i, slot_j):
         return xall.at[slot_j, pl.ds(i * tq, tq)]
 
@@ -122,6 +177,15 @@
 
         for k in range(1, r):
             rcopy(chunk(i, j), chunk(i, j), la_s.at[k, i], la_r.at[j, i], (q, g * r + lane(k))).start()
+    for k in range(1, nq):
+        s = rq(k)
+        rcopy(inv_all.at[s], inv_all.at[s], iv_s.at[k], iv_r.at[s], (s, c)).wait_recv()
+    inv_row = jnp.concatenate([inv_all[i] for i in range(nq)], axis=1)[:1]
+    inv_cols = []
+    for i in range(nq):
+        row = lax.broadcasted_iota(jnp.int32, (tq, total), 0) + i * tq
+        inv_cols.append(jnp.sum(jnp.where(pos == row, inv_row, 0.0), axis=1, keepdims=True))
+    inv = jnp.concatenate(inv_cols, axis=0)
     for i in range(nq):
         for k in range(1, r):
             s = lane(k)
@@ -130,12 +194,8 @@
     loads[0].wait()
     loads[1].wait()
 
-    sq = sum(jnp.sum(jnp.square(xall[i].astype(F32)), axis=1, keepdims=True) for i in range(r))
-    for i in range(nq):
-        ss_send[i] = jnp.broadcast_to(sq[i * tq:(i + 1) * tq], (tq, 128))
-    for k in range(1, nq):
-        d = rq(k)
-        rcopy(ss_send.at[d], ss_recv.at[q], ss_s.at[k], ss_r.at[q], (d, c)).start()
+    for i in range(r):
+        xn[i] = (xall[i].astype(F32) * inv).astype(BF16)
 
     def part_send(n, k):
         d = rq(k)
@@ -155,34 +215,30 @@
     def matmuls(n, carry):
         cols = pl.ds(pl.multiple_of(n * cw, cw), cw)
         for e, wref in enumerate((gate, up)):
-            full = sum(mm(xall[i], wref[i * w:(i + 1) * w, cols]) for i in range(r)).astype(BF16)
+            full = sum(mm(xn[i], wref[i * w:(i + 1) * w, cols]) for i in range(r))
             for i in range(nq):
-                psend[n, i, e] = full[i * tq:(i + 1) * tq]
+                psend[n, i, e] = full[i * tq:(i + 1) * tq].astype(BF16)
+
+                @pl.when(q == i)
+                def _(i=i, e=e, full=full):
+                    pown[n, e] = full[i * tq:(i + 1) * tq]
         for k in range(1, nq):
             part_send(n, k).start()
         return carry
 
     lax.fori_loop(0, nch, matmuls, 0)
 
-    ssum = ss_send[q]
-    for k in range(1, nq):
-        s = rq(k)
-        rcopy(ss_send.at[s], ss_recv.at[s], ss_s.at[k], ss_r.at[s], (s, c)).wait_recv()
-        ssum = ssum + ss_recv[s]
-    inv = lax.rsqrt(ssum[:, :1] / d_all + epsilon)
     loads[2].wait()
     acc[...] = jnp.zeros_like(acc)
 
     def reduce_chunk(n):
-        gsum = psend[n, q, 0].astype(F32)
-        usum = psend[n, q, 1].astype(F32)
+        gsum = pown[n, 0]
+        usum = pown[n, 1]
         for k in range(1, nq):
             part_recv(n, k).wait_recv()
             s = rq(k)
             gsum = gsum + precv[n, s, 0].astype(F32)
             usum = usum + precv[n, s, 1].astype(F32)
-        gsum = gsum * inv
-        usum = usum * inv
         hall[n, q] = (gsum / (1.0 + jnp.exp(-gsum)) * usum).astype(BF16)
         for k in range(1, nq):
             h_send(n, k).start()
@@ -289,11 +345,31 @@
         rcopy(codes.at[s], codes.at[s], o_s.at[k], o_r.at[s], (s, c)).wait_recv()
     qcodes = jnp.concatenate([codes[i] for i in range(nq)], axis=1)
     scale = 1.0 / math.sqrt(corp.shape[1])
-    out[...] = lax.dot_general(qcodes, corp[...], (((1,), (1,)), ((), ())), preferred_element_type=F32) * scale
+    scores = lax.dot_general(qcodes, corp[...], (((1,), (1,)), ((), ())), preferred_element_type=F32) * scale
+
+    blocks = corp.shape[0] // LANES
+    lists = jnp.concatenate([scores[:, i * LANES:(i + 1) * LANES] for i in range(blocks)], axis=0)
+    best = merge_all(sort_lanes(lists), nqueries, q >= nq // 2)
+    top_q[q] = best
+    for k in range(1, nq):
+        rcopy(top_q.at[q], top_q.at[q], tq_s.at[k], tq_r.at[q], (rq(k), c)).start()
+    for k in range(1, nq):
+        s = rq(k)
+        rcopy(top_q.at[s], top_q.at[s], tq_s.at[k], tq_r.at[s], (s, c)).wait_recv()
+    best = merge_all(top_q[...].reshape(nq * nqueries, LANES), nqueries, c >= nc // 2)
+    top_c[c] = best
+    for k in range(1, nc):
+        rcopy(top_c.at[c], top_c.at[c], tc_s.at[k], tc_r.at[c], (q, rc(k))).start()
+    for k in range(1, nc):
+        s = rc(k)
+        rcopy(top_c.at[s], top_c.at[s], tc_s.at[k], tc_r.at[s], (q, s)).wait_recv()
+    best = merge_all(top_c[...].reshape(nc * nqueries, LANES), nqueries, False)
+    out[...] = best[:, :TOPK]
 
     for k in range(1, nq):
         rcopy(lens, lens_all.at[q], l_s.at[k], l_r.at[q], (rq(k), c)).wait_send()
-        rcopy(ss_send.at[q], ss_recv.at[q], ss_s.at[k], ss_r.at[q], (rq(k), c)).wait_send()
+        rcopy(inv_all.at[q], inv_all.at[q], iv_s.at[k], iv_r.at[q], (rq(k), c)).wait_send()
+        rcopy(top_q.at[q], top_q.at[q], tq_s.at[k], tq_r.at[q], (rq(k), c)).wait_send()
         rcopy(t_send, t_recv.at[q], t_s.at[k], t_r.at[q], (rq(k), c)).wait_send()
         rcopy(codes.at[q], codes.at[q], o_s.at[k], o_r.at[q], (rq(k), c)).wait_send()
 
@@ -336,9 +412,11 @@
             rcopy(pblk, pblk, pb_s.at[k], pb_r, (rq(k), c)).wait_send()
     for k in range(1, nc):
         rcopy(cpart, crecv.at[c], c_s.at[k], c_r.at[c], (q, rc(k))).wait_send()
-
-
-def device_scores(nq, nc, hidden_in, lengths, gate_weight, up_weight, down_weight, code_weight, corpus_codes):
+        rcopy(st_send, st_recv.at[c], st_s.at[k], st_r.at[c], (q, rc(k))).wait_send()
+        rcopy(top_c.at[c], top_c.at[c], tc_s.at[k], tc_r.at[c], (q, rc(k))).wait_send()
+
+
+def per_device(nq, nc, hidden_in, lengths, gate_weight, up_weight, down_weight, code_weight, corpus_codes):
     slots, w = hidden_in.shape
     r = nc // nq
     nreal = nq * slots * REAL_NUM // REAL_DEN
@@ -357,13 +435,16 @@
         vm(code_weight.shape, BF16), vm(corpus_codes.shape, BF16),
         vm((nq, slots, w), BF16), vm((nq, 8, slots), jnp.int32), vm((r, nreal, w), BF16),
         vm((nch, nq, 2, tq, cw), BF16), vm((nch, nq, 2, tq, cw), BF16),
-        vm((nq, tq, 128), F32), vm((nq, tq, 128), F32), vm((nch, nq, tq, cw), BF16), vm((nreal, dq), F32),
+        vm((8, slots), F32), vm((nc, 8, slots), F32), vm((nq, 8, slots), F32), vm((r, nreal, w), BF16),
+        vm((nch, 2, tq, cw), F32), vm((nq, nqueries, LANES), F32), vm((nc, nqueries, LANES), F32),
+        vm((nch, nq, tq, cw), BF16), vm((nreal, dq), F32),
         vm((r, ng, tb, dq), BF16), vm((r, ng, tb, dq), BF16), vm((ng, tb, dq), BF16), vm((ng, tb, dq), BF16),
         vm((tb, 128), F32), vm((nq, tb, 128), F32),
         vm((r, nqueries, w), F32), vm((nc, nqueries, w), F32), vm((nqueries, w), BF16),
         vm((nqueries, bw), F32), vm((nc, nqueries, bw), F32), vm((nq, nqueries, bw), BF16),
         dma((5,)), dma, dma((nq,)), dma((nq,)), dma((nq,)), dma((2, nq)), dma((nq,)), dma((r, nq)), dma((r, nq)),
-        dma((nch, nq)), dma((nch, nq)), dma((nq,)), dma((nq,)), dma((nch, nq)), dma((nch, nq)),
+        dma((nch, nq)), dma((nch, nq)), dma((nc,)), dma((nc,)), dma((nq,)), dma((nq,)),
+        dma((nq,)), dma((nq,)), dma((nc,)), dma((nc,)), dma((nch, nq)), dma((nch, nq)),
         dma((r,)), dma((r,)), dma((ng,)), dma((ng,)), dma((nq,)), dma((nq,)),
         dma((r,)), dma((nc,)), dma((nq,)), dma, dma((nc,)), dma((nc,)), dma((nq,)), dma((nq,)),
     ]
@@ -371,25 +452,13 @@
     vspec, aspec = pl.BlockSpec(memory_space=pltpu.VMEM), pl.BlockSpec(memory_space=pl.ANY)
     return pl.pallas_call(
         functools.partial(block_kernel, dims),
-        out_shape=jax.ShapeDtypeStruct((nqueries, corpus_codes.shape[0]), F32),
+        out_shape=jax.ShapeDtypeStruct((nqueries, TOPK), F32),
         in_specs=[vspec, vspec] + [aspec] * 5,
         out_specs=vspec,
         scratch_shapes=scratch,
         compiler_params=pltpu.CompilerParams(
-            collective_id=0, has_side_effects=True, vmem_limit_bytes=48 * 1024 * 1024),
+            collective_id=0, has_side_effects=True, vmem_limit_bytes=60 * 1024 * 1024),
     )(hidden_in, lens, gate_weight, up_weight, down_weight, code_weight, corpus_codes)
-
-
-def per_device(nq, nc, *args):
-    scores = device_scores(nq, nc, *args)
-    local_best = lax.top_k(scores, min(TOPK, scores.shape[1]))[0]
-    if nq * nc * local_best.shape[1] > 4096:
-        local_best = lax.all_gather(local_best, "query", axis=1, tiled=True)
-        local_best = lax.top_k(local_best, TOPK)[0]
-        everyone = lax.all_gather(local_best, "corpus", axis=1, tiled=True)
-    else:
-        everyone = lax.all_gather(local_best, ("query", "corpus"), axis=1, tiled=True)
-    return lax.top_k(everyone, TOPK)[0]
 
 
 def solution(mesh):

time: 183 us -> 119 us (0.65)
  blocking collectives: 41.7 us -> 0 us
  other arithmetic: 31.9 us -> 0 us
  Pallas kernels: 102 us -> 117 us
  local copies, waits for them, and re-layouts: 7.1 us -> 2.7 us
    all_gather x1 -> x0, blocking collectives: 41.7 us -> none  [per_device(): lax.all_gather(local_best, ('query', 'corpus'), axis=1, tiled=True)]
    top_k x2 -> x0, other arithmetic: 31.9 us -> none  [the longest x1 28.8 us: per_device(): return lax.top_k(everyone, TOPK)[0]]
    pallas_call x1, Pallas kernels: 102 us -> 117 us  [per_device(): pl.pallas_call(functools.partial(block_kernel, dims), out_shape=jax.Shape...]
    unnamed x9 -> x1, local copies, waits for them, and re-layouts: 5.58 us -> 1.3 us
where the time goes in v2:
time: 119 us
  Pallas kernels  117 us (98%)
  local copies, waits for them, and re-layouts  2.7 us (2%)
    pallas_call x1, Pallas kernels, per_device(): pl.pallas_call(functools.partial(block_kernel, dims), out_shape=jax.Shape...  117 us

profile of v2, /device:TPU:0, one launch (start us, length us, event | category | flops | bytes accessed | tf_op | source)
XLA Modules:
  0.0 119.3 jit_solution(3578179583864857590)
XLA Ops:
  0.0 0.7 broadcast_in_dim.10
  0.7 0.1 broadcast_in_dim.11
  0.8 0.6 broadcast_in_dim.12.lens
  1.4 116.6 %shard_map.73 = f32[16,100]{1,0:T(8,128)} custom-call(bf16[128,512]{1,0:T(8,128)(2,1)} %hid.1, s32[8,128]{1,0:T(8,128)} %broadcast_in_dim.12.lens, bf16[1024,1792]{1,0:T(8,128)(2,1)} %gate_h.1, bf16[1024,1792]{1,0:T(8,128)(2,1)} %up_h.1, bf16[1792,1024]{1,0:T(8,128)(2,1)} %down_h.1, bf16[512,1024]{1,0:T(8,128)(2,1)} %code_h.1, bf16[512,1024]{1,0:T(8,128)(2,1)} %corp_h.1), custom_call_target="tpu_custom_call" | custom-call | tf_op jit(solution)/shard_map/pallas_call | solution.py:453
  118.0 1.3 %copy.9 = f32[16,100]{1,0:T(8,128)} copy(f32[16,100]{1,0:T(8,128)} %shard_map.73) | data formatting | bytes 12800

commit v3 on v2

--- a/solution.py
+++ b/solution.py
@@ -197,20 +197,41 @@
     for i in range(r):
         xn[i] = (xall[i].astype(F32) * inv).astype(BF16)
 
-    def part_send(n, k):
-        d = rq(k)
-        return rcopy(psend.at[n, d], precv.at[n, q], p_s.at[n, k], p_r.at[n, q], (d, c))
-
-    def part_recv(n, k):
-        s = rq(k)
-        return rcopy(psend.at[n, s], precv.at[n, s], p_s.at[n, k], p_r.at[n, s], (s, c))
-
-    def h_send(n, k):
-        return rcopy(hall.at[n, q], hall.at[n, q], h_s.at[n, k], h_r.at[n, q], (rq(k), c))
-
-    def h_recv(n, k):
-        s = rq(k)
-        return rcopy(hall.at[n, s], hall.at[n, s], h_s.at[n, k], h_r.at[n, s], (s, c))
+    side_a = q + 1 - 2 * lax.rem(q, 2)
+    side_b = q + 2 - 4 * (q // 2)
+    far = nq - 1 - q
+
+    def sides(n):
+        odd = lax.rem(n, 2)
+        return side_a + (side_b - side_a) * odd, side_b + (side_a - side_b) * odd
+
+    def near_part(n):
+        one, _ = sides(n)
+        return rcopy(psend.at[n, one], precv.at[n, 0], p_s.at[n, 0], p_r.at[n, 0], (one, c))
+
+    def far_part(n):
+        one, _ = sides(n)
+        return rcopy(psend.at[n, far], precv.at[n, 1], p_s.at[n, 1], p_r.at[n, 1], (one, c))
+
+    def passed_part(n):
+        _, two = sides(n)
+        return rcopy(precv.at[n, 3], precv.at[n, 2], p_s.at[n, 2], p_r.at[n, 2], (two, c))
+
+    def h_near(n, k):
+        to = sides(n)[k]
+        return rcopy(hall.at[n, q], hall.at[n, q], h_s.at[n, k], h_r.at[n, k], (to, c))
+
+    def h_near_in(n, k):
+        to = sides(n)[k]
+        return rcopy(hall.at[n, to], hall.at[n, to], h_s.at[n, k], h_r.at[n, k], (to, c))
+
+    def h_pass(n):
+        one, two = sides(n)
+        return rcopy(hall.at[n, one], hall.at[n, one], h_s.at[n, 2], h_r.at[n, 2], (two, c))
+
+    def h_pass_in(n):
+        _, two = sides(n)
+        return rcopy(hall.at[n, far], hall.at[n, far], h_s.at[n, 2], h_r.at[n, 2], (two, c))
 
     def matmuls(n, carry):
         cols = pl.ds(pl.multiple_of(n * cw, cw), cw)
@@ -222,8 +243,8 @@
                 @pl.when(q == i)
                 def _(i=i, e=e, full=full):
                     pown[n, e] = full[i * tq:(i + 1) * tq]
-        for k in range(1, nq):
-            part_send(n, k).start()
+        far_part(n).start()
+        near_part(n).start()
         return carry
 
     lax.fori_loop(0, nch, matmuls, 0)
@@ -231,32 +252,50 @@
     loads[2].wait()
     acc[...] = jnp.zeros_like(acc)
 
+    def pass_chunk(n):
+        _, two = sides(n)
+        far_part(n).wait_recv()
+        precv[n, 3] = (psend[n, two].astype(F32) + precv[n, 1].astype(F32)).astype(BF16)
+        passed_part(n).start()
+
     def reduce_chunk(n):
-        gsum = pown[n, 0]
-        usum = pown[n, 1]
-        for k in range(1, nq):
-            part_recv(n, k).wait_recv()
-            s = rq(k)
-            gsum = gsum + precv[n, s, 0].astype(F32)
-            usum = usum + precv[n, s, 1].astype(F32)
+        near_part(n).wait_recv()
+        passed_part(n).wait_recv()
+        gsum = pown[n, 0] + precv[n, 0, 0].astype(F32) + precv[n, 2, 0].astype(F32)
+        usum = pown[n, 1] + precv[n, 0, 1].astype(F32) + precv[n, 2, 1].astype(F32)
         hall[n, q] = (gsum / (1.0 + jnp.exp(-gsum)) * usum).astype(BF16)
-        for k in range(1, nq):
-            h_send(n, k).start()
+        h_near(n, 0).start()
+        h_near(n, 1).start()
+
+    def relay_chunk(n):
+        h_near_in(n, 0).wait_recv()
+        h_pass(n).start()
 
     def down_chunk(n):
-        for k in range(1, nq):
-            h_recv(n, k).wait_recv()
+        h_near_in(n, 1).wait_recv()
+        h_pass_in(n).wait_recv()
         acc[...] += mm(hall[n].reshape(nreal, cw), down[pl.ds(pl.multiple_of(n * cw, cw), cw), :])
 
+    def passes(n, carry):
+        pass_chunk(n)
+        return carry
+
+    lax.fori_loop(0, nch, passes, 0)
     reduce_chunk(0)
 
-    def both(n, carry):
+    def reduces(n, carry):
         reduce_chunk(n)
-        down_chunk(n - 1)
+        relay_chunk(n - 1)
         return carry
 
-    lax.fori_loop(1, nch, both, 0)
-    down_chunk(nch - 1)
+    lax.fori_loop(1, nch, reduces, 0)
+    relay_chunk(nch - 1)
+
+    def downs(n, carry):
+        down_chunk(n)
+        return carry
+
+    lax.fori_loop(0, nch, downs, 0)
 
     ng = nc // r
     for gg in range(ng):
@@ -390,9 +429,12 @@
             rcopy(chunk(i, j), chunk(i, j), la_s.at[k, i], la_r.at[j, i], (q, g * r + lane(k))).wait_send()
 
     def drain(n, carry):
-        for k in range(1, nq):
-            part_send(n, k).wait_send()
-            h_send(n, k).wait_send()
+        far_part(n).wait_send()
+        near_part(n).wait_send()
+        passed_part(n).wait_send()
+        h_near(n, 0).wait_send()
+        h_near(n, 1).wait_send()
+        h_pass(n).wait_send()
         return carry
 
     lax.fori_loop(0, nch, drain, 0)

time: 119 us -> 112 us (0.941)
  Pallas kernels: 117 us -> 110 us
    pallas_call x1, Pallas kernels: 117 us -> 110 us  [per_device(): pl.pallas_call(functools.partial(block_kernel, dims), out_shape=jax.Shape...]
where the time goes in v3:
time: 112 us
  Pallas kernels  110 us (98%)
  local copies, waits for them, and re-layouts  2.7 us (2%)
    pallas_call x1, Pallas kernels, per_device(): pl.pallas_call(functools.partial(block_kernel, dims), out_shape=jax.Shape...  110 us

profile of v3, /device:TPU:0, one launch (start us, length us, event | category | flops | bytes accessed | tf_op | source)
XLA Modules:
  0.0 112.3 jit_solution(12513204826160846077)
XLA Ops:
  0.0 0.7 broadcast_in_dim.10
  0.7 0.1 broadcast_in_dim.11
  0.8 0.6 broadcast_in_dim.12.lens
  1.4 109.6 %shard_map.73 = f32[16,100]{1,0:T(8,128)} custom-call(bf16[128,512]{1,0:T(8,128)(2,1)} %hid.1, s32[8,128]{1,0:T(8,128)} %broadcast_in_dim.12.lens, bf16[1024,1792]{1,0:T(8,128)(2,1)} %gate_h.1, bf16[1024,1792]{1,0:T(8,128)(2,1)} %up_h.1, bf16[1792,1024]{1,0:T(8,128)(2,1)} %down_h.1, bf16[512,1024]{1,0:T(8,128)(2,1)} %code_h.1, bf16[512,1024]{1,0:T(8,128)(2,1)} %corp_h.1), custom_call_target="tpu_custom_call" | custom-call | tf_op jit(solution)/shard_map/pallas_call | solution.py:495
  111.0 1.3 %copy.9 = f32[16,100]{1,0:T(8,128)} copy(f32[16,100]{1,0:T(8,128)} %shard_map.73) | data formatting | bytes 12800

commit v4 on v3

--- a/solution.py
+++ b/solution.py
@@ -13,6 +13,7 @@
 TOPK = 100
 REAL_NUM, REAL_DEN = 5, 8
 CHUNK = 256
+PIECE = 32
 
 epsilon = 1e-05
 F32, BF16 = jnp.float32, jnp.bfloat16
@@ -138,8 +139,11 @@
     for k in range(1, nq):
         rcopy(inv_all.at[q], inv_all.at[q], iv_s.at[k], iv_r.at[q], (rq(k), c)).start()
 
+    nb = ch_r.shape[0]
+    ct = nreal // nb
+
     def chunk(i, slot_j):
-        return xall.at[slot_j, pl.ds(i * tq, tq)]
+        return xall.at[slot_j, pl.ds(i * ct, ct)]
 
     def down_chain(i):
         return rcopy(chunk(i, j), chunk(i, j), ch_s.at[0, i], ch_r.at[i], (q, jnp.maximum(c - r, 0)))
@@ -162,7 +166,7 @@
             pick = (pos == row).astype(F32).astype(BF16)
             xall[j, i * tq:(i + 1) * tq, :] = mm(pick, stacked).astype(BF16)
 
-    for i in range(nq):
+    for i in range(nb):
         @pl.when(q != g)
         def _(i=i):
             up_chain(i).wait_recv()
@@ -186,7 +190,7 @@
         row = lax.broadcasted_iota(jnp.int32, (tq, total), 0) + i * tq
         inv_cols.append(jnp.sum(jnp.where(pos == row, inv_row, 0.0), axis=1, keepdims=True))
     inv = jnp.concatenate(inv_cols, axis=0)
-    for i in range(nq):
+    for i in range(nb):
         for k in range(1, r):
             s = lane(k)
             rcopy(chunk(i, s), chunk(i, s), la_s.at[k, i], la_r.at[s, i], (q, g * r + s)).wait_recv()
@@ -416,7 +420,7 @@
     def _():
         rcopy(hid, colbuf.at[q], a_s, a_r.at[q], (g, c)).wait_send()
 
-    for i in range(nq):
+    for i in range(nb):
         @pl.when(sends_up)
         def _(i=i):
             up_chain(i).wait_send()
@@ -466,6 +470,7 @@
     dq, ffc = gate_weight.shape
     cw = CHUNK if ffc % CHUNK == 0 else ffc
     nch = ffc // cw
+    nb = nreal // PIECE if nreal % PIECE == 0 else nq
     nqueries = nq * lengths.shape[0]
     bits = code_weight.shape[1]
     bw = bits // nq
@@ -484,7 +489,7 @@
         vm((tb, 128), F32), vm((nq, tb, 128), F32),
         vm((r, nqueries, w), F32), vm((nc, nqueries, w), F32), vm((nqueries, w), BF16),
         vm((nqueries, bw), F32), vm((nc, nqueries, bw), F32), vm((nq, nqueries, bw), BF16),
-        dma((5,)), dma, dma((nq,)), dma((nq,)), dma((nq,)), dma((2, nq)), dma((nq,)), dma((r, nq)), dma((r, nq)),
+        dma((5,)), dma, dma((nq,)), dma((nq,)), dma((nq,)), dma((2, nb)), dma((nb,)), dma((r, nb)), dma((r, nb)),
         dma((nch, nq)), dma((nch, nq)), dma((nc,)), dma((nc,)), dma((nq,)), dma((nq,)),
         dma((nq,)), dma((nq,)), dma((nc,)), dma((nc,)), dma((nch, nq)), dma((nch, nq)),
         dma((r,)), dma((r,)), dma((ng,)), dma((ng,)), dma((nq,)), dma((nq,)),

time: 112 us -> 111 us (level)
  Pallas kernels: 110 us -> 108 us
    pallas_call x1, Pallas kernels: 110 us -> 108 us  [per_device(): pl.pallas_call(functools.partial(block_kernel, dims), out_shape=jax.Shape...]
where the time goes in v4:
time: 111 us
  Pallas kernels  108 us (97%)
  local copies, waits for them, and re-layouts  2.7 us (2%)
    pallas_call x1, Pallas kernels, per_device(): pl.pallas_call(functools.partial(block_kernel, dims), out_shape=jax.Shape...  108 us

profile of v4, /device:TPU:0, one launch (start us, length us, event | category | flops | bytes accessed | tf_op | source)
XLA Modules:
  0.0 110.8 jit_solution(2649790571126254121)
XLA Ops:
  0.0 0.7 broadcast_in_dim.10
  0.7 0.1 broadcast_in_dim.11
  0.8 0.6 broadcast_in_dim.12.lens
  1.4 108.1 %shard_map.73 = f32[16,100]{1,0:T(8,128)} custom-call(bf16[128,512]{1,0:T(8,128)(2,1)} %hid.1, s32[8,128]{1,0:T(8,128)} %broadcast_in_dim.12.lens, bf16[1024,1792]{1,0:T(8,128)(2,1)} %gate_h.1, bf16[1024,1792]{1,0:T(8,128)(2,1)} %up_h.1, bf16[1792,1024]{1,0:T(8,128)(2,1)} %down_h.1, bf16[512,1024]{1,0:T(8,128)(2,1)} %code_h.1, bf16[512,1024]{1,0:T(8,128)(2,1)} %corp_h.1), custom_call_target="tpu_custom_call" | custom-call | tf_op jit(solution)/shard_map/pallas_call | solution.py:500
  109.5 1.3 %copy.9 = f32[16,100]{1,0:T(8,128)} copy(f32[16,100]{1,0:T(8,128)} %shard_map.73) | data formatting | bytes 12800
